TPU v7x, 32 devices: a whole 2x2x4 slice. The times are simulated.
32 devices in a mesh: grp: 2 (over y), vec: 4 (over z), occ: 2 (over x), wlk: 2 (over core).
Axes of the slice: x: 2, y: 2, z: 4, core: 2. Of those that a mesh axis runs over, the one named last changes fastest.
Arguments:
- chol_half: bfloat16 [256, 256, 2048], P(('grp', 'vec'), 'occ'), parts along dimension 0, may hold values from -0.046875 to 0.046875
- theta: bfloat16 [8, 2048, 256], P(('grp', 'wlk'), 'vec', 'occ'), parts along dimension 0, may hold values from -6 to 6
Outputs:
- theta_grad: float32 [8, 2048, 256], P(('grp', 'wlk'), 'vec', 'occ'), parts along dimension 0
There are 2 independent parts, one for each index of `grp`. A program takes and returns all parts, laid end to end along the dimension named above; each array names one. Nothing has to cross between parts.
All inputs are finite; a program needn't handle non-finite values.
Results may differ from a plain program's by a relative error of at most 0.0042.
Values may be sent and summed in bfloat16 or wider, within the bound.
No kernel may reach another device: no remote copies, remote signals or barrier semaphores. Data moves between devices by JAX's collectives and lax.ppermute only.
A program may use at most 64 MiB of HBM per device.

v0:
```python
import jax
import jax.numpy as jnp
from jax import lax
from jax.sharding import PartitionSpec as P


def on_device(chol_half, theta):
    widened = lax.all_gather(theta, "occ", axis=2, tiled=True)
    factor_rows = chol_half
    amplitude_sums = jnp.einsum(
        "gip,wpj->wgij",
        factor_rows,
        lax.all_gather(widened, "vec", axis=1, tiled=True),
        preferred_element_type=jnp.float32,
    )
    amplitudes = amplitude_sums.astype(jnp.bfloat16)
    swapped = lax.all_to_all(amplitudes, "occ", split_axis=3, concat_axis=2, tiled=True)
    factor_rows = chol_half
    summed_rows = lax.psum_scatter(
        jnp.einsum("gap,wgba->pwb", factor_rows, swapped, preferred_element_type=jnp.float32),
        "vec",
        scatter_dimension=0,
        tiled=True,
    )
    owned = lax.psum_scatter(summed_rows, "occ", scatter_dimension=2, tiled=True)
    return -jnp.transpose(owned, (1, 0, 2))


def solution(mesh):
    placed = (P(("grp", "vec"), "occ", None), P(("grp", "wlk"), "vec", "occ"))
    return jax.shard_map(
        on_device,
        mesh=mesh,
        in_specs=placed,
        out_specs=P(("grp", "wlk"), "vec", "occ"),
        check_vma=False,
    )
```

profile of v0, /device:TPU:0, one launch (start us, length us, event | category | flops | bytes accessed | tf_op | source)
XLA Modules:
  0.0 259.8 jit_solution(8337746905256795681)
XLA Ops:
  6.5 0.0 all-gather.2.cloned.1.call-start
  6.5 1.1 copy.6
  7.6 10.0 %all_gather.6 = bf16[2,512,256]{1,2,0:T(8,128)(2,1)} all-gather(bf16[2,512,128]{1,2,0:T(8,128)(2,1)S(1)} %copy.6), channel_id=1, replica_groups=mesh['grp'=2,'vec'=4,'occ'=2,'wlk'=2] {'occ'}, dimensions={2}, use_global_device_ids=true | all-gather | bytes 786432 | tf_op jit(solution)/shard_map/all_gather | solution.py:8
  17.7 0.0 all-gather.2.cloned.1.call-update
  17.7 0.0 reduce-scatter.3.cloned.1.call-start
  17.7 47.3 %all-gather.2.cloned.1.call-done = bf16[2,2048,256]{1,2,0:T(8,128)(2,1)} async-done(((bf16[2,512,256]{1,2,0:T(8,128)(2,1)}), bf16[2,2048,256]{1,2,0:T(8,128)(2,1)}) %all-gather.2.cloned.1.call-update) | async-done | bytes 2097168 | tf_op jit(solution)/shard_map/all_gather | solution.py:13
  65.0 12.4 %convert_bitcast_fusion = bf16[2,32,128,256]{2,3,1,0:T(8,128)(2,1)S(1)} fusion(bf16[32,128,2048]{2,1,0:T(8,128)(2,1)} %param.2, bf16[2,2048,256]{1,2,0:T(8,128)(2,1)} %all-gather.2.cloned.1.call-done), kind=kOutput, calls=%fused_computation.4 | convolution fusion | flops 8592031744 | bytes 23068672 | tf_op jit(solution)/shard_map/gip,wpj->wgij/dot_general | solution.py:10
  77.4 2.7 %copy.7 = bf16[2,32,128,256]{2,1,0,3:T(8,128)(2,1)S(1)} copy(bf16[2,32,128,256]{2,3,1,0:T(8,128)(2,1)S(1)} %convert_bitcast_fusion) | data formatting | bytes 8388608 | tf_op jit(solution)/shard_map/convert_element_type | solution.py:16
  80.1 51.1 %all_to_all.18 = bf16[2,32,128,256]{2,1,0,3:T(8,128)(2,1)} all-to-all(bf16[2,32,128,256]{2,1,0,3:T(8,128)(2,1)S(1)} %copy.7), channel_id=1, replica_groups=mesh['grp'=2,'vec'=4,'occ'=2,'wlk'=2] {'occ'}, dimensions={3} | all-to-all | bytes 8388608 | tf_op jit(solution)/shard_map/all_to_all | solution.py:17
  131.3 7.5 %copy.8 = bf16[2,32,128,2,128]{4,2,3,1,0:T(8,128)(2,1)} copy(bf16[2,32,128,2,128]{2,1,0,4,3:T(8,128)(2,1)} %bitcast.28) | data formatting | bytes 8388608 | tf_op jit(solution)/shard_map/all_to_all | solution.py:17
  138.8 14.1 %fusion.4 = f32[2048,2,256]{0,2,1:T(8,128)} fusion(bf16[2,32,256,128]{3,2,1,0:T(8,128)(2,1)} %bitcast.29, bf16[32,128,2048]{2,1,0:T(8,128)(2,1)} %param.2), kind=kOutput, calls=%fused_computation.5 | convolution fusion | flops 8589934592 | bytes 25165824 | tf_op jit(solution)/shard_map/gap,wgba->pwb/dot_general | solution.py:20
  152.9 0.0 reduce-scatter.3.cloned.1.call-update
  152.9 0.0 reduce-scatter.5.cloned.1.call-start
  153.0 75.0 %reduce-scatter.3.cloned.1.call-done = f32[512,2,256]{0,2,1:T(8,128)} async-done(((f32[2048,2,256]{0,2,1:T(8,128)}), f32[512,2,256]{0,2,1:T(8,128)}) %reduce-scatter.3.cloned.1.call-update) | async-done | bytes 1048592 | tf_op jit(solution)/shard_map/reduce_scatter | solution.py:19
  228.0 0.0 reduce-scatter.5.cloned.1.call-update
  228.0 23.1 %reduce-scatter.5.cloned.1.call-done = f32[512,2,128]{0,2,1:T(8,128)} async-done(((f32[512,2,256]{0,2,1:T(8,128)}), f32[512,2,128]{0,2,1:T(8,128)}) %reduce-scatter.5.cloned.1.call-update) | async-done | bytes 524304 | tf_op jit(solution)/shard_map/reduce_scatter | solution.py:25
  251.2 1.1 negate_bitcast_fusion
  252.3 1.0 copy.9
Async XLA Ops:
  6.5 58.5 %all-gather.2.cloned.1.call-start = ((), (), s32[]{:S(2)}) async-start(), calls=%async_computation.3 | async-start | bytes 2621440 | tf_op jit(solution)/shard_map/all_gather | solution.py:13
  17.7 210.3 %reduce-scatter.3.cloned.1.call-start = ((), (), s32[]{:S(2)}) async-start(), calls=%async_computation.4 | async-start | bytes 5242880 | tf_op jit(solution)/shard_map/reduce_scatter | solution.py:19
  152.9 98.2 %reduce-scatter.5.cloned.1.call-start = ((), (), s32[]{:S(2)}) async-start(), calls=%async_computation.5 | async-start | bytes 1572864 | tf_op jit(solution)/shard_map/reduce_scatter | solution.py:25
Sparse Core Ops, SparseCore 0:
  17.8 47.1 all-gather.1
  153.0 74.9 reduce-scatter.2
  230.2 20.8 reduce-scatter.4
where the time goes:
time: 260 us
  waiting for transfers between devices  145 us (56%)
  blocking collectives  61.2 us (24%)
  matrix products  26.5 us (10%)
  between operations  13.1 us (5%)
  local copies, waits for them, and re-layouts  12.3 us (5%)
    reduce_scatter x1, waiting for transfers between devices, on_device(): lax.psum_scatter(jnp.einsum('gap,wgba->pwb', factor_rows, swapped, prefer...  75 us
    all_to_all x1, blocking collectives, on_device(): lax.all_to_all(amplitudes, 'occ', split_axis=3, concat_axis=2, tiled=True)  51.1 us
    all_gather x1, waiting for transfers between devices, on_device(): lax.all_gather(widened, 'vec', axis=1, tiled=True)  47.3 us
    reduce_scatter x1, waiting for transfers between devices, on_device(): lax.psum_scatter(summed_rows, 'occ', scatter_dimension=2, tiled=True)  23.1 us
    dot_general x1, matrix products, on_device(): jnp.einsum('gap,wgba->pwb', factor_rows, swapped, preferred_element_type=...  14.1 us
    dot_general x1, matrix products, on_device(): jnp.einsum('gip,wpj->wgij', factor_rows, lax.all_gather(widened, 'vec', a...  12.4 us
    all_gather x1, blocking collectives, on_device(): widened = lax.all_gather(theta, 'occ', axis=2, tiled=True)  10 us
    all_to_all x1, local copies, waits for them, and re-layouts, on_device(): lax.all_to_all(amplitudes, 'occ', split_axis=3, concat_axis=2, tiled=True)  7.48 us
  transfers between devices with their start and end apart: 3, of which 3 were waited for; matrix products, arithmetic and copies ran while one was open for 0% of the time, Pallas kernels for 0%

commit v1 on v0

--- a/solution.py
+++ b/solution.py
@@ -10,7 +10,9 @@
     amplitude_sums = jnp.einsum(
         "gip,wpj->wgij",
         factor_rows,
-        lax.all_gather(widened, "vec", axis=1, tiled=True),
+        jnp.concatenate(
+            lax.all_to_all(jnp.stack([widened] * lax.axis_size("vec")), "vec", 0, 0), axis=1
+        ),
         preferred_element_type=jnp.float32,
     )
     amplitudes = amplitude_sums.astype(jnp.bfloat16)

time: 260 us -> 269 us (1.035)
  blocking collectives: 61.2 us -> 112 us
  waiting for transfers between devices: 145 us -> 99 us
  local copies, waits for them, and re-layouts: 12.3 us -> 16 us
    all_to_all x0 -> x1, blocking collectives: none -> 52.2 us  [on_device(): lax.all_to_all(jnp.stack([widened] * lax.axis_size('vec')), 'vec', 0, 0)]
    all_gather x1 -> x0, waiting for transfers between devices: 47.3 us -> none  [on_device(): lax.all_gather(widened, 'vec', axis=1, tiled=True)]
    reshape x0 -> x2, local copies, waits for them, and re-layouts: none -> 4.42 us  [on_device(): jnp.concatenate(lax.all_to_all(jnp.stack([widened] * lax.axis_size('vec')...]
  transfers between devices with their start and end apart: 3 -> 2, of which waited for: 3 -> 2; matrix products, arithmetic and copies ran while one was open for 0% -> 0% of each run, Pallas kernels for 0% -> 0%
where the time goes in v1:
time: 269 us
  blocking collectives  112 us (42%)
  waiting for transfers between devices  99 us (37%)
  matrix products  26.6 us (10%)
  local copies, waits for them, and re-layouts  16 us (6%)
  between operations  13.4 us (5%)
    reduce_scatter x1, waiting for transfers between devices, on_device(): lax.psum_scatter(jnp.einsum('gap,wgba->pwb', factor_rows, swapped, prefer...  75.8 us
    all_to_all x1, blocking collectives, on_device(): lax.all_to_all(jnp.stack([widened] * lax.axis_size('vec')), 'vec', 0, 0)  52.2 us
    all_to_all x1, blocking collectives, on_device(): lax.all_to_all(amplitudes, 'occ', split_axis=3, concat_axis=2, tiled=True)  50.1 us
    reduce_scatter x1, waiting for transfers between devices, on_device(): lax.psum_scatter(summed_rows, 'occ', scatter_dimension=2, tiled=True)  23.2 us
    dot_general x1, matrix products, on_device(): jnp.einsum('gap,wgba->pwb', factor_rows, swapped, preferred_element_type=...  14.2 us
    dot_general x1, matrix products, on_device(): jnp.einsum('gip,wpj->wgij', factor_rows, jnp.concatenate(lax.all_to_all(j...  12.4 us
    all_gather x1, blocking collectives, on_device(): widened = lax.all_gather(theta, 'occ', axis=2, tiled=True)  10.2 us
    all_to_all x1, local copies, waits for them, and re-layouts, on_device(): lax.all_to_all(amplitudes, 'occ', split_axis=3, concat_axis=2, tiled=True)  7.51 us
  transfers between devices with their start and end apart: 2, of which 2 were waited for; matrix products, arithmetic and copies ran while one was open for 0% of the time, Pallas kernels for 0%

profile of v1, /device:TPU:0, one launch (start us, length us, event | category | flops | bytes accessed | tf_op | source)
XLA Modules:
  0.0 268.6 jit_solution(12080509854704249515)
XLA Ops:
  6.5 0.0 reduce-scatter.3.cloned.1.call-start
  6.5 10.2 %all_gather.3 = bf16[2,512,256]{2,1,0:T(8,128)(2,1)S(1)} all-gather(bf16[2,512,128]{2,1,0:T(8,128)(2,1)} %param.3), channel_id=1, replica_groups=mesh['grp'=2,'vec'=4,'occ'=2,'wlk'=2] {'occ'}, dimensions={2}, use_global_device_ids=true | all-gather | bytes 786432 | tf_op jit(solution)/shard_map/all_gather | solution.py:8
  16.7 0.2 copy.6
  17.0 0.2 stack.2
  17.1 52.2 %all_to_all.23 = bf16[4,2,512,256]{2,3,1,0:T(8,128)(2,1)S(1)} all-to-all(bf16[4,2,512,256]{2,3,1,0:T(8,128)(2,1)S(1)} %stack.2), channel_id=1, replica_groups=mesh['grp'=2,'vec'=4,'occ'=2,'wlk'=2] {'vec'}, dimensions={0} | all-to-all | bytes 4194304 | tf_op jit(solution)/shard_map/all_to_all | solution.py:14
  69.3 1.6 copy.7
  71.0 2.8 %reshape.10 = bf16[2,2048,256,1]{1,2,0,3:T(8,128)(2,1)} reshape(bf16[2,4,512,256]{2,1,3,0:T(4,128)(2,1)S(1)} %copy.7) | data formatting | bytes 4194304 | tf_op jit(solution)/shard_map/reshape | solution.py:13
  73.8 12.4 %convert_bitcast_fusion = bf16[2,32,128,256]{2,3,1,0:T(8,128)(2,1)S(1)} fusion(bf16[32,128,2048]{2,1,0:T(8,128)(2,1)} %param.2, bf16[2,2048,256,1]{1,2,0,3:T(8,128)(2,1)} %reshape.10), kind=kOutput, calls=%fused_computation.4 | convolution fusion | flops 8592031744 | bytes 23068672 | tf_op jit(solution)/shard_map/gip,wpj->wgij/dot_general | solution.py:10
  86.2 2.7 %copy.8 = bf16[2,32,128,256]{2,1,0,3:T(8,128)(2,1)S(1)} copy(bf16[2,32,128,256]{2,3,1,0:T(8,128)(2,1)S(1)} %convert_bitcast_fusion) | data formatting | bytes 8388608 | tf_op jit(solution)/shard_map/convert_element_type | solution.py:18
  88.9 50.1 %all_to_all.24 = bf16[2,32,128,256]{2,1,0,3:T(8,128)(2,1)} all-to-all(bf16[2,32,128,256]{2,1,0,3:T(8,128)(2,1)S(1)} %copy.8), channel_id=1, replica_groups=mesh['grp'=2,'vec'=4,'occ'=2,'wlk'=2] {'occ'}, dimensions={3} | all-to-all | bytes 8388608 | tf_op jit(solution)/shard_map/all_to_all | solution.py:19
  139.0 7.5 %copy.9 = bf16[2,32,128,2,128]{4,2,3,1,0:T(8,128)(2,1)} copy(bf16[2,32,128,2,128]{2,1,0,4,3:T(8,128)(2,1)} %bitcast.29) | data formatting | bytes 8388608 | tf_op jit(solution)/shard_map/all_to_all | solution.py:19
  146.5 14.2 %fusion.4 = f32[2048,2,256]{0,2,1:T(8,128)} fusion(bf16[2,32,256,128]{3,2,1,0:T(8,128)(2,1)} %bitcast.31, bf16[32,128,2048]{2,1,0:T(8,128)(2,1)} %param.2), kind=kOutput, calls=%fused_computation.5 | convolution fusion | flops 8589934592 | bytes 25165824 | tf_op jit(solution)/shard_map/gap,wgba->pwb/dot_general | solution.py:22
  160.7 0.0 reduce-scatter.3.cloned.1.call-update
  160.7 0.0 reduce-scatter.5.cloned.1.call-start
  160.7 75.8 %reduce-scatter.3.cloned.1.call-done = f32[512,2,256]{0,2,1:T(8,128)} async-done(((f32[2048,2,256]{0,2,1:T(8,128)}), f32[512,2,256]{0,2,1:T(8,128)}) %reduce-scatter.3.cloned.1.call-update) | async-done | bytes 1048592 | tf_op jit(solution)/shard_map/reduce_scatter | solution.py:21
  236.5 0.0 reduce-scatter.5.cloned.1.call-update
  236.6 23.2 %reduce-scatter.5.cloned.1.call-done = f32[512,2,128]{0,2,1:T(8,128)} async-done(((f32[512,2,256]{0,2,1:T(8,128)}), f32[512,2,128]{0,2,1:T(8,128)}) %reduce-scatter.5.cloned.1.call-update) | async-done | bytes 524304 | tf_op jit(solution)/shard_map/reduce_scatter | solution.py:27
  259.7 1.1 negate_bitcast_fusion
  260.8 1.0 copy.10
Async XLA Ops:
  6.5 230.0 %reduce-scatter.3.cloned.1.call-start = ((), (), s32[]{:S(2)}) async-start(), calls=%async_computation.4 | async-start | bytes 5242880 | tf_op jit(solution)/shard_map/reduce_scatter | solution.py:21
  160.7 99.0 %reduce-scatter.5.cloned.1.call-start = ((), (), s32[]{:S(2)}) async-start(), calls=%async_computation.5 | async-start | bytes 1572864 | tf_op jit(solution)/shard_map/reduce_scatter | solution.py:27
Sparse Core Ops, SparseCore 0:
  160.8 75.6 reduce-scatter.2
  238.8 20.8 reduce-scatter.4
